TPU v7x, 128 devices: a whole 4x4x4 slice. The times are simulated.
128 devices in a mesh: gx: 16 (over y, x), gy: 4 (over z), gz: 2 (over core).
Axes of the slice: x: 4, y: 4, z: 4, core: 2. Of those that a mesh axis runs over, the one named last changes fastest.
Arguments:
- adjoint: float32 [5, 384, 64, 256], P(None, 'gx', 'gy', 'gz'), may hold values from -6 to 6
- base_density: float32 [384, 64, 256], P('gx', 'gy', 'gz'), may hold values from 0.5 to 2
- base_velocity: float32 [3, 384, 64, 256], P(None, 'gx', 'gy', 'gz'), may hold values from -2.5 to 2.5
- base_pressure: float32 [384, 64, 256], P('gx', 'gy', 'gz'), may hold values from 0.5 to 2
Outputs:
- tendency: float32 [5, 384, 64, 256], P(None, 'gx', 'gy', 'gz')
- updated: float32 [5, 384, 64, 256], P(None, 'gx', 'gy', 'gz')
All inputs are finite; a program needn't handle non-finite values.
Results may differ from a plain program's by a relative error of at most 0.0003.
Values sent between devices are 32-bit elements; how exact they have to be, the bound alone decides.
A program may use at most 192 MiB of HBM per device.

v0:
```python
import functools

import jax
import jax.numpy as jnp
import numpy as np
from jax import lax
from jax.experimental import pallas as pl
from jax.experimental.pallas import tpu as pltpu
from jax.sharding import PartitionSpec as P

GAMMA_LESS = 0.4
RATIO = 1.0 / 3.0
COEF_NEAR = 7.0 / 9.0
COEF_FAR = 1.0 / 36.0
RANK = 4
F32 = jnp.float32
BF16 = jnp.bfloat16


def derivative(total, periodic):
    eye = np.eye(total)
    if periodic:
        up1, lo1, up2, lo2 = (np.roll(eye, s, axis=1) for s in (1, -1, 2, -2))
    else:
        up1, lo1, up2, lo2 = (np.eye(total, k=s) for s in (1, -1, 2, -2))
    banded = eye + RATIO * (up1 + lo1)
    stencil = COEF_NEAR * (up1 - lo1) + COEF_FAR * (up2 - lo2)
    return -stencil @ np.linalg.inv(banded)


def stacked(matrix, rows, cols):
    return np.vstack([matrix[rows, cols], (matrix @ matrix)[rows, cols]])


def line_factors(block):
    long = derivative(9 * block, False)
    near = derivative(4 * block, False)
    own = slice(4 * block, 5 * block)
    local = stacked(long, own, own)
    sides = []
    for beside, edge in (
        (slice(3 * block, 4 * block), slice(0, block)),
        (slice(5 * block, 6 * block), slice(3 * block, 4 * block)),
    ):
        basis, size, functional = np.linalg.svd(stacked(long, own, beside))
        basis = basis[:, :RANK]
        sides.append(
            (basis, size[:RANK, None] * functional[:RANK], basis.T @ (stacked(near, edge, edge) - local))
        )
    return local, sides


def high_low(matrix, axis):
    high = matrix.astype(np.float32).astype(BF16)
    low = (matrix - high.astype(np.float64)).astype(np.float32).astype(BF16)
    return np.concatenate([high, low], axis=axis)


@functools.lru_cache(maxsize=None)
def tables(nx, ny, nz, cx):
    loc_x, side_x = line_factors(nx)
    loc_y, side_y = line_factors(ny)
    eye_x, eye_y, eye_c = np.eye(nx), np.eye(ny), np.eye(cx)
    local = np.stack(
        [
            high_low(m, 0)
            for m in (
                np.kron(loc_x[nx:], eye_y) + np.kron(eye_x, loc_y[ny:]),
                np.kron(loc_x[:nx], eye_y),
                np.kron(eye_x, loc_y[:ny]),
            )
        ]
    )
    state_y = np.stack(
        [
            np.stack([high_low(np.kron(eye_c, m), 0) for m in pair])
            for pair in ((side_y[1][1], side_y[0][2]), (side_y[0][1], side_y[1][2]))
        ]
    )
    state_x = np.stack(
        [
            np.stack([high_low(np.kron(m, eye_y), 0) for m in pair])
            for pair in ((side_x[1][1], side_x[0][2]), (side_x[0][1], side_x[1][2]))
        ]
    )
    correct = []
    for c in range(nx // cx):
        rows = slice(c * cx, (c + 1) * cx)
        of_y = [np.kron(eye_c, s[0][ny:]) for s in side_y], [np.kron(eye_c, s[0][:ny]) for s in side_y]
        of_x = (
            [np.kron(s[0][nx:][rows], eye_y) for s in side_x],
            [np.kron(s[0][:nx][rows], eye_y) for s in side_x],
        )
        none_y, none_x = [np.zeros_like(m) for m in of_y[0]], [np.zeros_like(m) for m in of_x[0]]
        whole = np.vstack(
            [
                np.hstack(of_y[0] + of_x[0]),
                np.hstack(none_y + of_x[1]),
                np.hstack(of_y[1] + none_x),
            ]
        )
        whole = np.hstack([whole, np.zeros((whole.shape[0], 256 - whole.shape[1]))])
        correct.append(high_low(whole, 0))
    span = derivative(2 * nz, True)
    both = np.hstack([span[:nz].T, (span @ span)[:nz].T])
    return local, state_y, state_x, np.stack(correct), high_low(both, 1)


def split(value):
    high = value.astype(BF16)
    low = (value - high.astype(F32)).astype(BF16)
    return high, low


def product(matrix, columns):
    full = jnp.dot(matrix, columns, preferred_element_type=F32)
    rows = full.shape[0] // 2
    return full[:rows, :128] + full[:rows, 128:] + full[rows:, :128]


def kernel(
    cx, counts,
    adj_hbm, rho_hbm, vel_hbm, pre_hbm, loc_hbm, sty_hbm, stx_hbm, cor_hbm, spn_hbm,
    out_hbm,
    adj, rho, vel, pre, loc, sty, stx, cor, spn,
    cols, other, ysend, yrecv, xsend, xrecv, twice, fx, fy, fz, out,
    in_sem, out_sem, ys_sem, yr_sem, xs_sem, xr_sem, zs_sem, zr_sem,
):
    gx, gy, gz = (lax.axis_index(n) for n in ("gx", "gy", "gz"))
    n_gx, n_gy = counts
    variables = adj.shape[0]
    rows_c = cx * 16
    chunks = adj.shape[1] // rows_c

    loads = [
        pltpu.make_async_copy(src, dst, in_sem.at[k])
        for k, (src, dst) in enumerate(
            ((adj_hbm, adj), (sty_hbm, sty), (stx_hbm, stx), (loc_hbm, loc), (spn_hbm, spn),
             (rho_hbm, rho), (vel_hbm, vel), (pre_hbm, pre), (cor_hbm, cor))
        )
    ]
    for load in loads:
        load.start()

    has = (gx > 0, gx < n_gx - 1, gy > 0, gy < n_gy - 1)
    to = ({"gx": gx - 1}, {"gx": gx + 1}, {"gy": gy - 1}, {"gy": gy + 1})
    partner = {"gz": 1 - gz}
    barrier = pltpu.get_barrier_semaphore()
    for there, where in zip(has, to):

        @pl.when(there)
        def _(where=where):
            pl.semaphore_signal(barrier, inc=1, device_id=where, device_id_type=pl.DeviceIdType.MESH)

    pl.semaphore_signal(barrier, inc=1, device_id=partner, device_id_type=pl.DeviceIdType.MESH)

    def remote(src, dst, send, recv, where):
        return pltpu.make_async_remote_copy(
            src_ref=src, dst_ref=dst, send_sem=send, recv_sem=recv,
            device_id=where, device_id_type=pl.DeviceIdType.MESH,
        )

    def y_copy(slot, c):
        return remote(
            ysend.at[slot, c], yrecv.at[1 - slot, c], ys_sem.at[slot, c], yr_sem.at[1 - slot, c], to[2 + slot]
        )

    def x_copy(slot):
        return remote(xsend.at[slot], xrecv.at[1 - slot], xs_sem.at[slot], xr_sem.at[1 - slot], to[slot])

    def z_copy(v):
        return remote(adj_hbm.at[v], other.at[v], zs_sem.at[v], zr_sem.at[v], partner)

    loads[0].wait()
    for v in range(variables):
        high, low = split(adj[v])
        cols[v, :, :128] = high
        cols[v, :, 128:] = low

    edge = tuple(jnp.where(there, 0, 1) for there in has)
    loads[1].wait()
    neighbours = sum(jnp.where(there, 1, 0) for there in has) + 1
    for c in range(chunks):

        for v in range(variables):
            block = cols[v, c * rows_c : (c + 1) * rows_c, :]
            for slot in range(2):
                ysend[slot, c, v] = product(sty[slot, edge[2 + slot]], block)
        if c == 0:
            pl.semaphore_wait(barrier, neighbours)
        for slot in range(2):

            @pl.when(has[2 + slot])
            def _(slot=slot):
                y_copy(slot, c).start()

            @pl.when(jnp.logical_not(has[2 + slot]))
            def _(slot=slot):
                yrecv[slot, c] = ysend[slot, c]

    loads[2].wait()

    @pl.loop(0, variables)
    def _(v):
        for slot in range(2):
            xsend[slot, v] = product(stx[slot, edge[slot]], cols[v])

    for slot in range(2):

        @pl.when(has[slot])
        def _(slot=slot):
            x_copy(slot).start()

        @pl.when(jnp.logical_not(has[slot]))
        def _(slot=slot):
            xrecv[slot] = xsend[slot]

    for v in range(variables):
        z_copy(v).start()

    loads[3].wait()

    @pl.loop(0, variables)
    def _(v):
        for kind, into in enumerate((twice, fx, fy)):
            into[v] = product(loc[kind], cols[v])

    loads[4].wait()
    for v in range(variables):
        z_copy(v).wait_recv()

    @pl.loop(0, variables)
    def _(v):
        high, low = split(other[v])
        high = jnp.concatenate([cols[v, :, :128], high], axis=1)
        low = jnp.concatenate([cols[v, :, 128:], low], axis=1)
        width = spn.shape[1] // 2
        full = (
            jnp.dot(high, spn[:, :width], preferred_element_type=F32)
            + jnp.dot(low, spn[:, :width], preferred_element_type=F32)
            + jnp.dot(high, spn[:, width:], preferred_element_type=F32)
        )
        fz[v] = full[:, :128]
        twice[v] += full[:, 128:]

    for load in loads[5:]:
        load.wait()
    for slot in range(2):

        @pl.when(has[slot])
        def _(slot=slot):
            x_copy(1 - slot).wait_recv()

    zeros = jnp.zeros((256 - 2 * RANK * (cx + 16), 128), F32)
    writes = []
    for c in range(chunks):
        rows = pl.ds(c * rows_c, rows_c)
        for slot in range(2):

            @pl.when(has[2 + slot])
            def _(slot=slot):
                y_copy(1 - slot, c).wait_recv()

        @pl.loop(0, variables)
        def _(v):
            states = jnp.concatenate(
                [yrecv[0, c, v], yrecv[1, c, v], xrecv[0, v], xrecv[1, v], zeros], axis=0
            )
            high, low = split(states)
            change = product(cor[c], jnp.concatenate([high, low], axis=1))
            twice[v, rows] += change[:rows_c]
            fx[v, rows] += change[rows_c : 2 * rows_c]
            fy[v, rows] += change[2 * rows_c :]

        @pl.loop(0, rows_c // 16)
        def _(tile):
            at = pl.ds(pl.multiple_of(c * rows_c + tile * 16, 16), 16)
            density = rho[at]
            speed = [vel[d, at] for d in range(3)]
            square = 0.5 * (speed[0] * speed[0] + speed[1] * speed[1] + speed[2] * speed[2])
            enthalpy = (1.0 + 1.0 / GAMMA_LESS) * pre[at] / density + square
            first = [[f[v, at] for v in range(5)] for f in (fx, fy, fz)]
            heads = [
                g[1] * speed[0] + g[2] * speed[1] + g[3] * speed[2] + enthalpy * g[4] for g in first
            ]
            push = sum(g[1 + d] + speed[d] * g[4] for d, g in enumerate(first)) * GAMMA_LESS

            def carried(v):
                return speed[0] * first[0][v] + speed[1] * first[1][v] + speed[2] * first[2][v]

            conv = [
                square * push - (speed[0] * heads[0] + speed[1] * heads[1] + speed[2] * heads[2])
            ]
            for d in range(3):
                conv.append(carried(1 + d) + (first[d][0] + heads[d]) - speed[d] * push)
            conv.append(carried(4) + push)
            for v in range(5):
                out[v, at] = twice[v, at] - 2.0 * conv[v]

        write = pltpu.make_async_copy(out.at[:, rows], out_hbm.at[:, rows], out_sem.at[c])
        write.start()
        writes.append(write)

    for slot in range(2):
        for c in range(chunks):

            @pl.when(has[2 + slot])
            def _(slot=slot, c=c):
                y_copy(slot, c).wait_send()

        @pl.when(has[slot])
        def _(slot=slot):
            x_copy(slot).wait_send()

    for v in range(variables):
        z_copy(v).wait_send()
    for write in writes:
        write.wait()


def on_device(counts, adjoint, base_density, base_velocity, base_pressure):
    variables, nx, ny, nz = adjoint.shape
    cx = 8
    chunks = nx // cx
    rows = nx * ny
    local, state_y, state_x, correct, span = tables(nx, ny, nz, cx)
    field = (variables, rows, nz)
    y_shape = (2, chunks, variables, RANK * cx, nz)
    x_shape = (2, variables, RANK * ny, nz)
    dma = pltpu.SemaphoreType.DMA
    twice = pl.pallas_call(
        functools.partial(kernel, cx, counts),
        out_shape=jax.ShapeDtypeStruct(field, F32),
        in_specs=[pl.BlockSpec(memory_space=pl.ANY)] * 9,
        out_specs=pl.BlockSpec(memory_space=pl.ANY),
        scratch_shapes=[
            pltpu.VMEM(field, F32),
            pltpu.VMEM((rows, nz), F32),
            pltpu.VMEM((3, rows, nz), F32),
            pltpu.VMEM((rows, nz), F32),
            pltpu.VMEM(local.shape, BF16),
            pltpu.VMEM(state_y.shape, BF16),
            pltpu.VMEM(state_x.shape, BF16),
            pltpu.VMEM(correct.shape, BF16),
            pltpu.VMEM(span.shape, BF16),
            pltpu.VMEM((variables, rows, 2 * nz), BF16),
            pltpu.VMEM(field, F32),
            pltpu.VMEM(y_shape, F32),
            pltpu.VMEM(y_shape, F32),
            pltpu.VMEM(x_shape, F32),
            pltpu.VMEM(x_shape, F32),
            pltpu.VMEM(field, F32),
            pltpu.VMEM(field, F32),
            pltpu.VMEM(field, F32),
            pltpu.VMEM(field, F32),
            pltpu.VMEM(field, F32),
            dma((9,)),
            dma((chunks,)),
            dma((2, chunks)),
            dma((2, chunks)),
            dma((2,)),
            dma((2,)),
            dma((variables,)),
            dma((variables,)),
        ],
        compiler_params=pltpu.CompilerParams(
            collective_id=0, has_side_effects=True, vmem_limit_bytes=40 << 20
        ),
        name="adjoint_step",
    )(
        adjoint.reshape(field),
        base_density.reshape(rows, nz),
        base_velocity.reshape(3, rows, nz),
        base_pressure.reshape(rows, nz),
        local, state_y, state_x, correct, span,
    ).reshape(adjoint.shape)
    return 0.5 * twice, adjoint + 0.25 * twice


def solution(mesh):
    placed = (
        P(None, "gx", "gy", "gz"),
        P("gx", "gy", "gz"),
        P(None, "gx", "gy", "gz"),
        P("gx", "gy", "gz"),
    )
    return jax.shard_map(
        functools.partial(on_device, (mesh.shape["gx"], mesh.shape["gy"])),
        mesh=mesh,
        in_specs=placed,
        out_specs=(P(None, "gx", "gy", "gz"), P(None, "gx", "gy", "gz")),
        check_vma=False,
    )
```

profile of v0, /device:TPU:24, one launch (start us, length us, event | category | flops | bytes accessed | tf_op | source)
XLA Modules:
  0.0 29.9 jit_solution(11174190638612551382)
XLA Ops:
  0.6 0.0 copy-start
  0.6 1.2 %copy-done = f32[5,24,16,128]{3,2,1,0:T(8,128)S(1)} copy-done((f32[5,24,16,128]{3,2,1,0:T(8,128)S(1)}, f32[5,24,16,128]{3,2,1,0:T(8,128)}, u32[]{:S(2)}) %copy-start) | copy-done | bytes 983064
  1.8 0.0 copy-start.1
  1.8 1.5 %copy-done.1 = bf16[3,768,384]{2,1,0:T(8,128)(2,1)S(1)} copy-done((bf16[3,768,384]{2,1,0:T(8,128)(2,1)S(1)}, bf16[3,768,384]{2,1,0:T(8,128)(2,1)}, u32[]{:S(2)}) %copy-start.1) | copy-done | bytes 1769496
  3.3 0.0 copy-start.2
  3.3 1.3 %copy-done.2 = bf16[3,768,256]{2,1,0:T(8,128)(2,1)S(1)} copy-done((bf16[3,768,256]{2,1,0:T(8,128)(2,1)S(1)}, bf16[3,768,256]{2,1,0:T(8,128)(2,1)}, u32[]{:S(2)}) %copy-start.2) | copy-done | bytes 1179672
  4.6 0.0 copy-start.3
  4.6 1.1 %copy-done.3 = f32[3,24,16,128]{3,2,1,0:T(8,128)S(1)} copy-done((f32[3,24,16,128]{3,2,1,0:T(8,128)S(1)}, f32[3,24,16,128]{3,2,1,0:T(8,128)}, u32[]{:S(2)}) %copy-start.3) | copy-done | bytes 589848
  5.6 0.0 copy-start.4
  5.6 1.0 %copy-done.4 = bf16[2,2,128,384]{3,2,1,0:T(8,128)(2,1)S(1)} copy-done((bf16[2,2,128,384]{3,2,1,0:T(8,128)(2,1)S(1)}, bf16[2,2,128,384]{3,2,1,0:T(8,128)(2,1)}, u32[]{:S(2)}) %copy-start.4) | copy-done | bytes 393240
  6.6 0.0 copy-start.5
  6.6 0.9 %copy-done.5 = bf16[256,512]{1,0:T(8,128)(2,1)S(1)} copy-done((bf16[256,512]{1,0:T(8,128)(2,1)S(1)}, bf16[256,512]{1,0:T(8,128)(2,1)}, u32[]{:S(2)}) %copy-start.5) | copy-done | bytes 262168
  7.6 0.0 copy-start.6
  7.6 0.9 %copy-done.6 = f32[24,16,128]{2,1,0:T(8,128)S(1)} copy-done((f32[24,16,128]{2,1,0:T(8,128)S(1)}, f32[24,16,128]{2,1,0:T(8,128)}, u32[]{:S(2)}) %copy-start.6) | copy-done | bytes 196632
  8.5 0.0 copy-start.7
  8.5 0.9 %copy-done.7 = f32[24,16,128]{2,1,0:T(8,128)S(1)} copy-done((f32[24,16,128]{2,1,0:T(8,128)S(1)}, f32[24,16,128]{2,1,0:T(8,128)}, u32[]{:S(2)}) %copy-start.7) | copy-done | bytes 196632
  9.4 0.0 copy-start.8
  9.4 0.8 %copy-done.8 = bf16[2,2,64,128]{3,2,1,0:T(8,128)(2,1)S(1)} copy-done((bf16[2,2,64,128]{3,2,1,0:T(8,128)(2,1)S(1)}, bf16[2,2,64,128]{3,2,1,0:T(8,128)(2,1)}, u32[]{:S(2)}) %copy-start.8) | copy-done | bytes 65560
  10.3 17.5 %adjoint_step.1 = f32[5,384,128]{2,1,0:T(8,128)S(1)} custom-call(f32[5,384,128]{2,1,0:T(8,128)S(1)} %bitcast.6, f32[384,128]{1,0:T(8,128)S(1)} %bitcast.8, f32[3,384,128]{2,1,0:T(8,128)S(1)} %bitcast.7, f32[384,128]{1,0:T(8,128)S(1)} %bitcast.9, bf16[3,768,384]{2,1,0:T(8,128)(2,1)S(1)} %copy-done.1, bf16[2,2,64,128]{3,2,1,0:T(8,128)(2,1)S(1)} %copy-done.8, ...), custom_call_target="tpu_custom_call" | custom-call | tf_op jit(solution)/shard_map/adjoint_step/pallas_call | solution.py:331
  27.8 1.1 %broadcast_multiply_fusion = (f32[5,384,128]{2,1,0:T(8,128)S(1)}, f32[5,384,128]{2,1,0:T(8,128)}) fusion(f32[5,384,128]{2,1,0:T(8,128)S(1)} %adjoint_step.1), kind=kLoop, calls=%fused_computation | loop fusion | flops 491520 | bytes 2949120 | tf_op jit(solution)/shard_map/mul | solution.py:377
  28.9 1.1 %add.3 = f32[5,24,16,128]{3,2,1,0:T(8,128)} add(f32[5,24,16,128]{3,2,1,0:T(8,128)S(1)} %copy-done, f32[5,24,16,128]{3,2,1,0:T(8,128)S(1)} %bitcast.10) | non-fusion elementwise | flops 245760 | bytes 2949120 | tf_op jit(solution)/shard_map/add | solution.py:377
Async XLA Ops:
  0.6 1.2 %copy-start = (f32[5,24,16,128]{3,2,1,0:T(8,128)S(1)}, f32[5,24,16,128]{3,2,1,0:T(8,128)}, u32[]{:S(2)}) copy-start(f32[5,24,16,128]{3,2,1,0:T(8,128)} %param.9) | copy-start | bytes 2949124
  1.8 1.5 %copy-start.1 = (bf16[3,768,384]{2,1,0:T(8,128)(2,1)S(1)}, bf16[3,768,384]{2,1,0:T(8,128)(2,1)}, u32[]{:S(2)}) copy-start(bf16[3,768,384]{2,1,0:T(8,128)(2,1)} %constant.14.clone.loc_hbm) | copy-start | bytes 5308420
  3.3 1.3 %copy-start.2 = (bf16[3,768,256]{2,1,0:T(8,128)(2,1)S(1)}, bf16[3,768,256]{2,1,0:T(8,128)(2,1)}, u32[]{:S(2)}) copy-start(bf16[3,768,256]{2,1,0:T(8,128)(2,1)} %constant.17.clone.cor_hbm) | copy-start | bytes 3538948
  4.6 1.1 %copy-start.3 = (f32[3,24,16,128]{3,2,1,0:T(8,128)S(1)}, f32[3,24,16,128]{3,2,1,0:T(8,128)}, u32[]{:S(2)}) copy-start(f32[3,24,16,128]{3,2,1,0:T(8,128)} %param.11) | copy-start | bytes 1769476
  5.6 1.0 %copy-start.4 = (bf16[2,2,128,384]{3,2,1,0:T(8,128)(2,1)S(1)}, bf16[2,2,128,384]{3,2,1,0:T(8,128)(2,1)}, u32[]{:S(2)}) copy-start(bf16[2,2,128,384]{3,2,1,0:T(8,128)(2,1)} %constant.16.clone.stx_hbm) | copy-start | bytes 1179652
  6.6 0.9 %copy-start.5 = (bf16[256,512]{1,0:T(8,128)(2,1)S(1)}, bf16[256,512]{1,0:T(8,128)(2,1)}, u32[]{:S(2)}) copy-start(bf16[256,512]{1,0:T(8,128)(2,1)} %constant.18.clone.spn_hbm) | copy-start | bytes 786436
  7.6 0.9 %copy-start.6 = (f32[24,16,128]{2,1,0:T(8,128)S(1)}, f32[24,16,128]{2,1,0:T(8,128)}, u32[]{:S(2)}) copy-start(f32[24,16,128]{2,1,0:T(8,128)} %param.10) | copy-start | bytes 589828
  8.5 0.9 %copy-start.7 = (f32[24,16,128]{2,1,0:T(8,128)S(1)}, f32[24,16,128]{2,1,0:T(8,128)}, u32[]{:S(2)}) copy-start(f32[24,16,128]{2,1,0:T(8,128)} %param.12) | copy-start | bytes 589828
  9.4 0.8 %copy-start.8 = (bf16[2,2,64,128]{3,2,1,0:T(8,128)(2,1)S(1)}, bf16[2,2,64,128]{3,2,1,0:T(8,128)(2,1)}, u32[]{:S(2)}) copy-start(bf16[2,2,64,128]{3,2,1,0:T(8,128)(2,1)} %constant.15.clone.sty_hbm) | copy-start | bytes 196612
where the time goes:
time: 30.4 us; the launch traced here: 29.9 us
  Pallas kernels  17.5 us (58%)
  local copies, waits for them, and re-layouts  9.64 us (32%)
  other arithmetic  2.17 us (7%)
  between operations  0.66 us (2%)
    pallas_call x1, Pallas kernels, on_device(): pl.pallas_call(functools.partial(kernel, cx, counts), out_shape=jax.Shape...  17.5 us
    unnamed x18, local copies, waits for them, and re-layouts  9.64 us
    mul x1, other arithmetic, on_device(): return (0.5 * twice, adjoint + 0.25 * twice)  1.1 us
    add x1, other arithmetic, on_device(): return (0.5 * twice, adjoint + 0.25 * twice)  1.07 us

commit v1 on v0

v1 whole, which is shorter than its diff:
```python
import functools

import jax
import jax.numpy as jnp
import numpy as np
from jax import lax
from jax.experimental import pallas as pl
from jax.experimental.pallas import tpu as pltpu
from jax.sharding import PartitionSpec as P

GAMMA_LESS = 0.4
RATIO = 1.0 / 3.0
COEF_NEAR = 7.0 / 9.0
COEF_FAR = 1.0 / 36.0
RANK = 4
F32 = jnp.float32
BF16 = jnp.bfloat16


def derivative(total, periodic):
    eye = np.eye(total)
    if periodic:
        up1, lo1, up2, lo2 = (np.roll(eye, s, axis=1) for s in (1, -1, 2, -2))
    else:
        up1, lo1, up2, lo2 = (np.eye(total, k=s) for s in (1, -1, 2, -2))
    banded = eye + RATIO * (up1 + lo1)
    stencil = COEF_NEAR * (up1 - lo1) + COEF_FAR * (up2 - lo2)
    return -stencil @ np.linalg.inv(banded)


def stacked(matrix, rows, cols):
    return np.vstack([(matrix @ matrix)[rows, cols], -2.0 * matrix[rows, cols]])


def line_factors(block):
    long = derivative(9 * block, False)
    near = derivative(4 * block, False)
    own = slice(4 * block, 5 * block)
    local = stacked(long, own, own)
    sides = []
    for beside, edge in (
        (slice(3 * block, 4 * block), slice(0, block)),
        (slice(5 * block, 6 * block), slice(3 * block, 4 * block)),
    ):
        basis, size, functional = np.linalg.svd(stacked(long, own, beside))
        basis = basis[:, :RANK]
        sides.append(
            (basis, size[:RANK, None] * functional[:RANK], basis.T @ (stacked(near, edge, edge) - local))
        )
    return local, sides


def four(matrix):
    high = matrix.astype(np.float32).astype(BF16)
    low = (matrix - high.astype(np.float64)).astype(np.float32).astype(BF16)
    return np.concatenate([high, high, low, low], axis=1)


def direction(block, lines):
    local, sides = line_factors(block)
    eye = np.eye(lines)
    state = np.stack(
        [
            np.stack([four(np.kron(eye, m)) for m in pair])
            for pair in ((sides[1][1], sides[0][2]), (sides[0][1], sides[1][2]))
        ]
    )
    whole = four(np.vstack([np.kron(eye, local[:block]), np.kron(eye, local[block:])]))
    change = four(
        np.vstack(
            [np.hstack([np.kron(eye, s[0][part]) for s in sides]) for part in (slice(0, block), slice(block, None))]
        )
    )
    return state, whole, change


@functools.lru_cache(maxsize=None)
def tables(nx, ny, nz):
    span = derivative(2 * nz, True)
    both = np.hstack([(span @ span)[:nz].T, -2.0 * span[:nz].T])
    high = both.astype(np.float32).astype(BF16)
    low = (both - high.astype(np.float64)).astype(np.float32).astype(BF16)
    return (*direction(ny, 4), *direction(nx, 2), np.stack([high, low]))


def split(value):
    high = value.astype(BF16)
    return high, (value - high.astype(F32)).astype(BF16)


def column(high, low):
    return jnp.concatenate([high, low, high, low], axis=0)


def dot(a, b):
    return jnp.dot(a, b, preferred_element_type=F32)


def pull(first, d, speed, square, enthalpy):
    head = first[1] * speed[0] + first[2] * speed[1] + first[3] * speed[2] + enthalpy * first[4]
    push = GAMMA_LESS * (first[1 + d] + speed[d] * first[4])
    result = [square * push - speed[d] * head]
    for i in range(3):
        term = speed[d] * first[1 + i] - speed[i] * push
        result.append(term + (first[0] + head) if i == d else term)
    result.append(speed[d] * first[4] + push)
    return result


def kernel(
    counts,
    adj_hbm, rho_hbm, vel_hbm, pre_hbm, sty_hbm, loy_hbm, chy_hbm, stx_hbm, lox_hbm, chx_hbm, spn_hbm,
    out_hbm,
    adj, rho, vel, pre, sty, loy, chy, stx, lox, chx, spn,
    highs, lows, other, ysend, yrecv, xsend, xrecv, twice, fy, tx, fx, squares, heats, out,
    adj_sem, in_sem, out_sem, ys_sem, yr_sem, xs_sem, xr_sem, zs_sem, zr_sem,
):
    gx, gy, gz = (lax.axis_index(n) for n in ("gx", "gy", "gz"))
    n_gx, n_gy = counts
    variables, rows_all, nz = adj.shape
    chunks = ysend.shape[1]
    rows_c = rows_all // chunks
    half = rows_c // 2
    ny = 16
    nx = rows_all // ny

    pieces = [
        pltpu.make_async_copy(
            adj_hbm.at[:, pl.ds(c * rows_c, rows_c)], adj.at[:, pl.ds(c * rows_c, rows_c)], adj_sem.at[c]
        )
        for c in range(chunks)
    ]
    loads = [
        pltpu.make_async_copy(src, dst, in_sem.at[k])
        for k, (src, dst) in enumerate(
            ((sty_hbm, sty), (loy_hbm, loy), (stx_hbm, stx), (lox_hbm, lox), (spn_hbm, spn),
             (rho_hbm, rho), (vel_hbm, vel), (pre_hbm, pre), (chx_hbm, chx), (chy_hbm, chy))
        )
    ]
    for load in pieces[:1] + loads[:2] + pieces[1:] + loads[2:]:
        load.start()

    has = (gx > 0, gx < n_gx - 1, gy > 0, gy < n_gy - 1)
    edge = tuple(jnp.where(there, 0, 1) for there in has)
    to = ({"gx": gx - 1}, {"gx": gx + 1}, {"gy": gy - 1}, {"gy": gy + 1})
    partner = {"gz": 1 - gz}
    barrier = pltpu.get_barrier_semaphore()
    for there, where in zip(has, to):

        @pl.when(there)
        def _(where=where):
            pl.semaphore_signal(barrier, inc=1, device_id=where, device_id_type=pl.DeviceIdType.MESH)

    pl.semaphore_signal(barrier, inc=1, device_id=partner, device_id_type=pl.DeviceIdType.MESH)
    neighbours = sum(jnp.where(there, 1, 0) for there in has) + 1

    def remote(src, dst, send, recv, where):
        return pltpu.make_async_remote_copy(
            src_ref=src, dst_ref=dst, send_sem=send, recv_sem=recv,
            device_id=where, device_id_type=pl.DeviceIdType.MESH,
        )

    def y_copy(slot, c):
        return remote(
            ysend.at[slot, c], yrecv.at[1 - slot, c], ys_sem.at[slot, c], yr_sem.at[1 - slot, c], to[2 + slot]
        )

    def x_copy(slot, v):
        return remote(
            xsend.at[slot, v], xrecv.at[1 - slot, v], xs_sem.at[slot, v], xr_sem.at[1 - slot, v], to[slot]
        )

    def z_copy(v):
        return remote(adj_hbm.at[v], other.at[v], zs_sem.at[v], zr_sem.at[v], partner)

    def y_part(c):
        rows = pl.ds(c * rows_c, rows_c)
        left = jnp.concatenate([sty[0, edge[2]], sty[1, edge[3]], loy[...]], axis=0)
        k = sty.shape[2]
        for v in range(variables):
            high, low = split(adj[v, rows])
            highs[v, rows] = high
            lows[v, rows] = low
            right = jnp.concatenate([column(high[:half], low[:half]), column(high[half:], low[half:])], axis=1)
            full = dot(left, right)
            for b in range(2):
                lanes = slice(b * nz, (b + 1) * nz)
                to_rows = pl.ds(c * rows_c + b * half, half)
                ysend[0, c, v, b] = full[:k, lanes]
                ysend[1, c, v, b] = full[k : 2 * k, lanes]
                twice[v, to_rows] = full[2 * k : 2 * k + half, lanes]
                fy[v, to_rows] = full[2 * k + half :, lanes]
        if c == 0:
            pl.semaphore_wait(barrier, neighbours)
        for slot in range(2):

            @pl.when(has[2 + slot])
            def _(slot=slot):
                y_copy(slot, c).start()

            @pl.when(jnp.logical_not(has[2 + slot]))
            def _(slot=slot):
                yrecv[slot, c] = ysend[slot, c]

    pieces[0].wait()
    loads[0].wait()
    loads[1].wait()
    y_part(0)
    for v in range(variables):
        z_copy(v).start()
    for c in range(1, chunks):
        pieces[c].wait()
    loads[2].wait()
    loads[3].wait()

    @pl.loop(0, variables)
    def _(v):
        left = jnp.concatenate([stx[0, edge[0]], stx[1, edge[1]], lox[...]], axis=0)
        k = stx.shape[2]
        for q in range(ny // 4):
            columns = []
            for b in range(2):
                lines = [adj[v, pl.ds(4 * q + 2 * b + j, nx, stride=ny)] for j in range(2)]
                columns.append(column(*split(jnp.concatenate(lines, axis=0))))
            full = dot(left, jnp.concatenate(columns, axis=1))
            for b in range(2):
                lanes = slice(b * nz, (b + 1) * nz)
                to_rows = pl.ds((4 * q + 2 * b) * nx, 2 * nx)
                xsend[0, v, 2 * q + b] = full[:k, lanes]
                xsend[1, v, 2 * q + b] = full[k : 2 * k, lanes]
                tx[v, to_rows] = full[2 * k : 2 * k + 2 * nx, lanes]
                fx[v, to_rows] = full[2 * k + 2 * nx :, lanes]
        for slot in range(2):

            @pl.when(has[slot])
            def _(slot=slot):
                x_copy(slot, v).start()

            @pl.when(jnp.logical_not(has[slot]))
            def _(slot=slot):
                xrecv[slot, v] = xsend[slot, v]

    for c in range(1, chunks):
        y_part(c)

    for load in loads[4:]:
        load.wait()
    for v in range(variables):
        z_copy(v).wait_recv()

    @pl.loop(0, variables)
    def _(v):
        high, low = split(other[v])
        high = jnp.concatenate([highs[v], high], axis=1)
        low = jnp.concatenate([lows[v], low], axis=1)
        full = dot(high, spn[0]) + dot(low, spn[0]) + dot(high, spn[1])
        twice[v] += full[:, :nz]
        other[v] = full[:, nz:]

    tile = 2 * ny

    @pl.loop(0, rows_all // tile)
    def _(t):
        at = pl.ds(pl.multiple_of(t * tile, tile), tile)
        speed = [vel[d, at] for d in range(3)]
        square = 0.5 * (speed[0] * speed[0] + speed[1] * speed[1] + speed[2] * speed[2])
        heat = (1.0 + 1.0 / GAMMA_LESS) * pre[at] / rho[at] + square
        squares[at] = square
        heats[at] = heat
        gained = pull([other[v, at] for v in range(5)], 2, speed, square, heat)
        for v in range(5):
            twice[v, at] += gained[v]

    @pl.loop(0, variables)
    def _(v):
        for slot in range(2):

            @pl.when(has[slot])
            def _(slot=slot):
                x_copy(1 - slot, v).wait_recv()

        for q in range(ny // 4):
            columns = [
                column(*split(jnp.concatenate([xrecv[slot, v, 2 * q + b] for slot in range(2)], axis=0)))
                for b in range(2)
            ]
            full = dot(chx[...], jnp.concatenate(columns, axis=1))
            for b in range(2):
                lanes = slice(b * nz, (b + 1) * nz)
                to_rows = pl.ds((4 * q + 2 * b) * nx, 2 * nx)
                tx[v, to_rows] += full[: 2 * nx, lanes]
                fx[v, to_rows] += full[2 * nx :, lanes]

    writes = []
    for c in range(chunks):
        rows = pl.ds(c * rows_c, rows_c)
        for slot in range(2):

            @pl.when(has[2 + slot])
            def _(slot=slot):
                y_copy(1 - slot, c).wait_recv()

        for v in range(variables):
            columns = [
                column(*split(jnp.concatenate([yrecv[slot, c, v, b] for slot in range(2)], axis=0)))
                for b in range(2)
            ]
            full = dot(chy[...], jnp.concatenate(columns, axis=1))
            for b in range(2):
                lanes = slice(b * nz, (b + 1) * nz)
                to_rows = pl.ds(c * rows_c + b * half, half)
                twice[v, to_rows] += full[:half, lanes]
                fy[v, to_rows] += full[half:, lanes]

        @pl.loop(0, rows_c // tile)
        def _(t):
            at = pl.ds(pl.multiple_of(c * rows_c + t * tile, tile), tile)
            first_line = c * (rows_c // ny) + t * (tile // ny)

            def turned(ref, v):
                return jnp.concatenate(
                    [ref[v, pl.ds(first_line + j, ny, stride=nx)] for j in range(tile // ny)], axis=0
                )

            speed = [vel[d, at] for d in range(3)]
            square, heat = squares[at], heats[at]
            by_x = pull([turned(fx, v) for v in range(5)], 0, speed, square, heat)
            by_y = pull([fy[v, at] for v in range(5)], 1, speed, square, heat)
            for v in range(5):
                out[v, at] = (twice[v, at] + turned(tx, v)) + (by_x[v] + by_y[v])

        write = pltpu.make_async_copy(out.at[:, rows], out_hbm.at[:, rows], out_sem.at[c])
        write.start()
        writes.append(write)

    for slot in range(2):
        for c in range(chunks):

            @pl.when(has[2 + slot])
            def _(slot=slot, c=c):
                y_copy(slot, c).wait_send()

        for v in range(variables):

            @pl.when(has[slot])
            def _(slot=slot, v=v):
                x_copy(slot, v).wait_send()

    for v in range(variables):
        z_copy(v).wait_send()
    for write in writes:
        write.wait()


def finish(twice_hbm, adj_hbm, tendency_hbm, updated_hbm, twice, adj, tendency, updated, in_sem, out_sem):
    variables = twice.shape[0]
    loads = [
        [
            pltpu.make_async_copy(twice_hbm.at[v], twice.at[v], in_sem.at[0, v]),
            pltpu.make_async_copy(adj_hbm.at[v], adj.at[v], in_sem.at[1, v]),
        ]
        for v in range(variables)
    ]
    for pair in loads:
        for load in pair:
            load.start()
    writes = []
    for v in range(variables):
        for load in loads[v]:
            load.wait()
        tendency[v] = 0.5 * twice[v]
        updated[v] = adj[v] + 0.25 * twice[v]
        for k, (src, dst) in enumerate(((tendency, tendency_hbm), (updated, updated_hbm))):
            write = pltpu.make_async_copy(src.at[v], dst.at[v], out_sem.at[k, v])
            write.start()
            writes.append(write)
    for write in writes:
        write.wait()


def on_device(counts, adjoint, base_density, base_velocity, base_pressure):
    variables, nx, ny, nz = adjoint.shape
    chunks = 3
    rows = nx * ny
    operators = tables(nx, ny, nz)
    field = (variables, rows, nz)
    y_shape = (2, chunks, variables, 2, 4 * RANK, nz)
    x_shape = (2, variables, ny // 2, 2 * RANK, nz)
    dma = pltpu.SemaphoreType.DMA
    hbm = pl.BlockSpec(memory_space=pl.ANY)
    whole = pltpu.VMEM(field, F32)
    whole_low = pltpu.VMEM(field, BF16)
    cells = pltpu.VMEM((rows, nz), F32)
    flat = adjoint.reshape(field)
    twice = pl.pallas_call(
        functools.partial(kernel, counts),
        out_shape=jax.ShapeDtypeStruct(field, F32),
        in_specs=[hbm] * 11,
        out_specs=hbm,
        scratch_shapes=[
            whole,
            cells,
            pltpu.VMEM((3, rows, nz), F32),
            cells,
            *[pltpu.VMEM(m.shape, BF16) for m in operators],
            whole_low,
            whole_low,
            whole,
            pltpu.VMEM(y_shape, F32),
            pltpu.VMEM(y_shape, F32),
            pltpu.VMEM(x_shape, F32),
            pltpu.VMEM(x_shape, F32),
            whole,
            whole,
            whole,
            whole,
            cells,
            cells,
            whole,
            dma((chunks,)),
            dma((10,)),
            dma((chunks,)),
            dma((2, chunks)),
            dma((2, chunks)),
            dma((2, variables)),
            dma((2, variables)),
            dma((variables,)),
            dma((variables,)),
        ],
        compiler_params=pltpu.CompilerParams(
            collective_id=0, has_side_effects=True, vmem_limit_bytes=62 << 20
        ),
        name="adjoint_step",
    )(
        flat,
        base_density.reshape(rows, nz),
        base_velocity.reshape(3, rows, nz),
        base_pressure.reshape(rows, nz),
        *operators,
    )
    tendency, updated = pl.pallas_call(
        finish,
        out_shape=[jax.ShapeDtypeStruct(field, F32)] * 2,
        in_specs=[hbm] * 2,
        out_specs=[hbm] * 2,
        scratch_shapes=[whole] * 4 + [dma((2, variables))] * 2,
        compiler_params=pltpu.CompilerParams(vmem_limit_bytes=62 << 20),
        name="finish",
    )(twice, flat)
    return tendency.reshape(adjoint.shape), updated.reshape(adjoint.shape)


def solution(mesh):
    placed = (
        P(None, "gx", "gy", "gz"),
        P("gx", "gy", "gz"),
        P(None, "gx", "gy", "gz"),
        P("gx", "gy", "gz"),
    )
    return jax.shard_map(
        functools.partial(on_device, (mesh.shape["gx"], mesh.shape["gy"])),
        mesh=mesh,
        in_specs=placed,
        out_specs=(P(None, "gx", "gy", "gz"), P(None, "gx", "gy", "gz")),
        check_vma=False,
    )
```

time: 30.4 us -> 16 us (0.53)
  local copies, waits for them, and re-layouts: 9.64 us -> 0 us
  Pallas kernels: 17.5 us -> 15.2 us
  other arithmetic: 2.17 us -> 0 us
    unnamed x18 -> x0, local copies, waits for them, and re-layouts: 9.64 us -> none
    pallas_call x1 -> x2, Pallas kernels: 17.5 us -> 15.2 us  [the longest x1 12.6 us: on_device(): pl.pallas_call(functools.partial(kernel, counts), out_shape=jax.ShapeDtyp...]
    mul x1 -> x0, other arithmetic: 1.1 us -> none  [on_device(): return (0.5 * twice, adjoint + 0.25 * twice)]
    add x1 -> x0, other arithmetic: 1.07 us -> none  [on_device(): return (0.5 * twice, adjoint + 0.25 * twice)]
where the time goes in v1:
time: 16 us; the launch traced here: 15.8 us
  Pallas kernels  15.2 us (95%)
  between operations  0.64 us (4%)
    pallas_call x1, Pallas kernels, on_device(): pl.pallas_call(functools.partial(kernel, counts), out_shape=jax.ShapeDtyp...  12.6 us
    pallas_call x1, Pallas kernels, on_device(): pl.pallas_call(finish, out_shape=[jax.ShapeDtypeStruct(field, F32)] * 2,...  2.54 us

profile of v1, /device:TPU:24, one launch (start us, length us, event | category | flops | bytes accessed | tf_op | source)
XLA Modules:
  0.0 15.8 jit_solution(4406580276278429539)
XLA Ops:
  0.6 12.6 %adjoint_step.1.twice_hbm = f32[5,384,128]{2,1,0:T(8,128)} custom-call(f32[5,384,128]{2,1,0:T(8,128)} %bitcast.6, f32[384,128]{1,0:T(8,128)} %bitcast.9, f32[3,384,128]{2,1,0:T(8,128)} %bitcast.8, f32[384,128]{1,0:T(8,128)} %bitcast.10, bf16[2,2,16,256]{3,2,1,0:T(8,128)(2,1)} %constant.14.clone.sty_hbm, bf16[128,256]{1,0:T(8,128)(2,1)} %constant.15.clone.loy_hbm, ...), custom_call_target="tpu_custom_call" | custom-call | tf_op jit(solution)/shard_map/adjoint_step/pallas_call | solution.py:395
  13.3 2.5 %finish.1 = (f32[5,384,128]{2,1,0:T(8,128)}, f32[5,384,128]{2,1,0:T(8,128)}) custom-call(f32[5,384,128]{2,1,0:T(8,128)} %adjoint_step.1.twice_hbm, f32[5,384,128]{2,1,0:T(8,128)} %bitcast.7), custom_call_target="tpu_custom_call" | custom-call | tf_op jit(solution)/shard_map/finish/pallas_call | solution.py:441

commit v2 on v1

--- a/solution.py
+++ b/solution.py
@@ -110,10 +110,10 @@
 def kernel(
     counts,
     adj_hbm, rho_hbm, vel_hbm, pre_hbm, sty_hbm, loy_hbm, chy_hbm, stx_hbm, lox_hbm, chx_hbm, spn_hbm,
-    out_hbm,
+    tendency, updated,
     adj, rho, vel, pre, sty, loy, chy, stx, lox, chx, spn,
-    highs, lows, other, ysend, yrecv, xsend, xrecv, twice, fy, tx, fx, squares, heats, out,
-    adj_sem, in_sem, out_sem, ys_sem, yr_sem, xs_sem, xr_sem, zs_sem, zr_sem,
+    highs, lows, other, ysend, yrecv, xsend, xrecv, twice, fy, tx, fx, squares, heats,
+    adj_sem, in_sem, ys_sem, yr_sem, xs_sem, xr_sem, zs_sem, zr_sem,
 ):
     gx, gy, gz = (lax.axis_index(n) for n in ("gx", "gy", "gz"))
     n_gx, n_gy = counts
@@ -291,9 +291,7 @@
                 tx[v, to_rows] += full[: 2 * nx, lanes]
                 fx[v, to_rows] += full[2 * nx :, lanes]
 
-    writes = []
     for c in range(chunks):
-        rows = pl.ds(c * rows_c, rows_c)
         for slot in range(2):
 
             @pl.when(has[2 + slot])
@@ -327,11 +325,9 @@
             by_x = pull([turned(fx, v) for v in range(5)], 0, speed, square, heat)
             by_y = pull([fy[v, at] for v in range(5)], 1, speed, square, heat)
             for v in range(5):
-                out[v, at] = (twice[v, at] + turned(tx, v)) + (by_x[v] + by_y[v])
-
-        write = pltpu.make_async_copy(out.at[:, rows], out_hbm.at[:, rows], out_sem.at[c])
-        write.start()
-        writes.append(write)
+                total = (twice[v, at] + turned(tx, v)) + (by_x[v] + by_y[v])
+                tendency[v, at] = 0.5 * total
+                updated[v, at] = adj[v, at] + 0.25 * total
 
     for slot in range(2):
         for c in range(chunks):
@@ -348,32 +344,15 @@
 
     for v in range(variables):
         z_copy(v).wait_send()
+
+
+def finish(tendency, updated, tendency_hbm, updated_hbm, sem):
+    writes = [
+        pltpu.make_async_copy(src, dst, sem.at[k])
+        for k, (src, dst) in enumerate(((tendency, tendency_hbm), (updated, updated_hbm)))
+    ]
     for write in writes:
-        write.wait()
-
-
-def finish(twice_hbm, adj_hbm, tendency_hbm, updated_hbm, twice, adj, tendency, updated, in_sem, out_sem):
-    variables = twice.shape[0]
-    loads = [
-        [
-            pltpu.make_async_copy(twice_hbm.at[v], twice.at[v], in_sem.at[0, v]),
-            pltpu.make_async_copy(adj_hbm.at[v], adj.at[v], in_sem.at[1, v]),
-        ]
-        for v in range(variables)
-    ]
-    for pair in loads:
-        for load in pair:
-            load.start()
-    writes = []
-    for v in range(variables):
-        for load in loads[v]:
-            load.wait()
-        tendency[v] = 0.5 * twice[v]
-        updated[v] = adj[v] + 0.25 * twice[v]
-        for k, (src, dst) in enumerate(((tendency, tendency_hbm), (updated, updated_hbm))):
-            write = pltpu.make_async_copy(src.at[v], dst.at[v], out_sem.at[k, v])
-            write.start()
-            writes.append(write)
+        write.start()
     for write in writes:
         write.wait()
 
@@ -391,12 +370,11 @@
     whole = pltpu.VMEM(field, F32)
     whole_low = pltpu.VMEM(field, BF16)
     cells = pltpu.VMEM((rows, nz), F32)
-    flat = adjoint.reshape(field)
-    twice = pl.pallas_call(
+    tendency, updated = pl.pallas_call(
         functools.partial(kernel, counts),
-        out_shape=jax.ShapeDtypeStruct(field, F32),
+        out_shape=[pltpu.VMEM(field, F32)] * 2,
         in_specs=[hbm] * 11,
-        out_specs=hbm,
+        out_specs=[pl.BlockSpec(memory_space=pltpu.VMEM)] * 2,
         scratch_shapes=[
             whole,
             cells,
@@ -416,10 +394,8 @@
             whole,
             cells,
             cells,
-            whole,
             dma((chunks,)),
             dma((10,)),
-            dma((chunks,)),
             dma((2, chunks)),
             dma((2, chunks)),
             dma((2, variables)),
@@ -428,25 +404,30 @@
             dma((variables,)),
         ],
         compiler_params=pltpu.CompilerParams(
-            collective_id=0, has_side_effects=True, vmem_limit_bytes=62 << 20
+            collective_id=0, has_side_effects=True, vmem_limit_bytes=32 << 20
         ),
         name="adjoint_step",
     )(
-        flat,
-        base_density.reshape(rows, nz),
-        base_velocity.reshape(3, rows, nz),
-        base_pressure.reshape(rows, nz),
-        *operators,
+        *[
+            pltpu.with_memory_space_constraint(jnp.asarray(x), pltpu.HBM)
+            for x in (
+                adjoint.reshape(field),
+                base_density.reshape(rows, nz),
+                base_velocity.reshape(3, rows, nz),
+                base_pressure.reshape(rows, nz),
+                *operators,
+            )
+        ]
     )
     tendency, updated = pl.pallas_call(
         finish,
         out_shape=[jax.ShapeDtypeStruct(field, F32)] * 2,
-        in_specs=[hbm] * 2,
+        in_specs=[pl.BlockSpec(memory_space=pltpu.VMEM)] * 2,
         out_specs=[hbm] * 2,
-        scratch_shapes=[whole] * 4 + [dma((2, variables))] * 2,
-        compiler_params=pltpu.CompilerParams(vmem_limit_bytes=62 << 20),
+        scratch_shapes=[dma((2,))],
+        compiler_params=pltpu.CompilerParams(vmem_limit_bytes=16 << 20),
         name="finish",
-    )(twice, flat)
+    )(*[pltpu.with_memory_space_constraint(x, pltpu.VMEM) for x in (tendency, updated)])
     return tendency.reshape(adjoint.shape), updated.reshape(adjoint.shape)
 
 

time: 16 us -> 14 us (0.88)
  Pallas kernels: 15.2 us -> 13.2 us
    pallas_call x1, Pallas kernels: 2.54 us -> 1.29 us  [on_device(): pl.pallas_call(finish, out_shape=[jax.ShapeDtypeStruct(field, F32)] * 2,...]
    pallas_call x1, Pallas kernels: 12.6 us -> 12 us  [on_device(): pl.pallas_call(functools.partial(kernel, counts), out_shape=[pltpu.VMEM(f...]
where the time goes in v2:
time: 14 us; the launch traced here: 13.9 us
  Pallas kernels  13.2 us (94%)
  between operations  0.64 us (5%)
    pallas_call x1, Pallas kernels, on_device(): pl.pallas_call(functools.partial(kernel, counts), out_shape=[pltpu.VMEM(f...  12 us
    pallas_call x1, Pallas kernels, on_device(): pl.pallas_call(finish, out_shape=[jax.ShapeDtypeStruct(field, F32)] * 2,...  1.29 us

profile of v2, /device:TPU:24, one launch (start us, length us, event | category | flops | bytes accessed | tf_op | source)
XLA Modules:
  0.0 13.9 jit_solution(9068676699784166683)
XLA Ops:
  0.6 12.0 %adjoint_step.1 = (f32[5,384,128]{2,1,0:T(8,128)S(1)}, f32[5,384,128]{2,1,0:T(8,128)S(1)}) custom-call(f32[5,384,128]{2,1,0:T(8,128)} %bitcast.6, f32[384,128]{1,0:T(8,128)} %bitcast.8, f32[3,384,128]{2,1,0:T(8,128)} %bitcast.7, f32[384,128]{1,0:T(8,128)} %bitcast.9, bf16[2,2,16,256]{3,2,1,0:T(8,128)(2,1)} %constant.14.clone.sty_hbm, ...), custom_call_target="tpu_custom_call" | custom-call | tf_op jit(solution)/shard_map/adjoint_step/pallas_call | solution.py:373
  12.6 1.3 %finish.1 = (f32[5,384,128]{2,1,0:T(8,128)}, f32[5,384,128]{2,1,0:T(8,128)}) custom-call(f32[5,384,128]{2,1,0:T(8,128)S(1)} %get-tuple-element.6.tendency, f32[5,384,128]{2,1,0:T(8,128)S(1)} %get-tuple-element.7.updated), custom_call_target="tpu_custom_call" | custom-call | tf_op jit(solution)/shard_map/finish/pallas_call | solution.py:422

commit v3 on v2

v3 whole, which is shorter than its diff:
```python
import functools

import jax
import jax.numpy as jnp
import numpy as np
from jax import lax
from jax.experimental import pallas as pl
from jax.experimental.pallas import tpu as pltpu
from jax.sharding import PartitionSpec as P

GAMMA_LESS = 0.4
RATIO = 1.0 / 3.0
COEF_NEAR = 7.0 / 9.0
COEF_FAR = 1.0 / 36.0
RANK = 4
THIN = True
SENT = 24 if THIN else 32
EDGE = 16
F32 = jnp.float32
BF16 = jnp.bfloat16


def derivative(total, periodic):
    eye = np.eye(total)
    if periodic:
        up1, lo1, up2, lo2 = (np.roll(eye, s, axis=1) for s in (1, -1, 2, -2))
    else:
        up1, lo1, up2, lo2 = (np.eye(total, k=s) for s in (1, -1, 2, -2))
    banded = eye + RATIO * (up1 + lo1)
    stencil = COEF_NEAR * (up1 - lo1) + COEF_FAR * (up2 - lo2)
    return -stencil @ np.linalg.inv(banded)


def stacked(matrix, rows, cols):
    return np.vstack([(matrix @ matrix)[rows, cols], -2.0 * matrix[rows, cols]])


def line_factors(block, thin):
    long = derivative(9 * block, False)
    near = derivative(4 * block, False)
    own = slice(4 * block, 5 * block)
    local = stacked(long, own, own)
    sides = []
    for beside, edge in (
        (slice(3 * block, 4 * block), slice(0, block)),
        (slice(5 * block, 6 * block), slice(3 * block, 4 * block)),
    ):
        basis, size, functional = np.linalg.svd(stacked(long, own, beside))
        basis, size, functional = basis[:, :RANK], size[:RANK], functional[:RANK]
        end = (basis, basis.T @ (stacked(near, edge, edge) - local))
        if thin:
            flat = functional.sum(axis=1)
            unseen = np.eye(RANK)[-1] - flat * flat[-1] / (flat @ flat)
            left_out = unseen / size**2
            left_out /= unseen @ left_out
            kept = np.linalg.svd(left_out[None])[2][1:].T
            basis, mixed = np.linalg.qr((basis * size) @ (np.eye(RANK) - np.outer(left_out, unseen)) @ kept)
            sides.append(((basis, mixed @ kept.T @ functional), end))
        else:
            sides.append(((basis, size[:, None] * functional), end))
    return local, sides


def four(matrix):
    high = matrix.astype(np.float32).astype(BF16)
    low = (matrix - high.astype(np.float64)).astype(np.float32).astype(BF16)
    return np.concatenate([high, high, low, low], axis=1)


def direction(block, lines, thin):
    local, sides = line_factors(block, thin)
    eye = np.eye(lines)
    order = [(slice(0, 2), slice(2, 3), slice(2, 3) if thin else slice(3, 4)), (slice(0, 2), slice(2, 3), slice(3, 4))]
    state = np.stack(
        [
            np.stack(
                [
                    four(np.vstack([np.kron(eye, factors[1][part]) for part in order[end]]))
                    for end, factors in enumerate(pair)
                ]
            )
            for pair in ((sides[1][0], sides[0][1]), (sides[0][0], sides[1][1]))
        ]
    )
    whole = four(np.vstack([np.kron(eye, local[:block]), np.kron(eye, local[block:])]))

    def gained(ends):
        return np.vstack(
            [
                np.hstack(
                    [np.kron(eye, side[end][0][half, part]) for side, end in zip(sides, ends) for part in order[end]]
                )
                for half in (slice(0, block), slice(block, None))
            ]
        )

    change = np.stack([np.stack([four(gained((a, b))) for b in range(2)]) for a in range(2)])
    both = np.concatenate([np.broadcast_to(whole, change.shape[:2] + whole.shape), change], axis=-1)
    return state, whole, change, both


def span_table(nz):
    span = derivative(2 * nz, True)
    both = np.hstack([(span @ span)[:nz].T, -2.0 * span[:nz].T])
    high = both.astype(np.float32).astype(BF16)
    low = (both - high.astype(np.float64)).astype(np.float32).astype(BF16)
    first, last = [nz + k for k in range(EDGE)], [2 * nz - EDGE + k for k in range(EDGE)]
    rest = np.zeros((nz - 6 * EDGE, 2 * nz), BF16)
    second = np.concatenate(
        [low[:nz], high[first], high[last], high[first], low[last], low[first], rest, high[last]], axis=0
    )
    return np.stack([np.concatenate([high[:nz], high[:nz]], axis=0), second])


@functools.lru_cache(maxsize=None)
def tables(nx, ny, nz):
    state_y, local_y, change_y, _ = direction(ny, 4, THIN)
    state_x, _, _, both_x = direction(nx, 2, False)
    return state_y, local_y, change_y, state_x, both_x, span_table(nz)


def split(value):
    high = value.astype(BF16)
    return high, (value - high.astype(F32)).astype(BF16)


def column(high, low):
    return jnp.concatenate([high, low, high, low], axis=0)


def dot(a, b):
    return jnp.dot(a, b, preferred_element_type=F32)


def pull(first, d, speed, square, enthalpy):
    head = first[1] * speed[0] + first[2] * speed[1] + first[3] * speed[2] + enthalpy * first[4]
    push = GAMMA_LESS * (first[1 + d] + speed[d] * first[4])
    result = [square * push - speed[d] * head]
    for i in range(3):
        term = speed[d] * first[1 + i] - speed[i] * push
        result.append(term + (first[0] + head) if i == d else term)
    result.append(speed[d] * first[4] + push)
    return result


def pull_two(g, k, speed, square, enthalpy):
    head_g = g[1] * speed[0] + g[2] * speed[1] + g[3] * speed[2] + enthalpy * g[4]
    head_k = k[1] * speed[0] + k[2] * speed[1] + k[3] * speed[2] + enthalpy * k[4]
    energy = speed[0] * g[4] + speed[1] * k[4]
    push = GAMMA_LESS * ((g[1] + k[2]) + energy)
    return [
        square * push - (speed[0] * head_g + speed[1] * head_k),
        (speed[0] * (g[1] - push) + speed[1] * k[1]) + (g[0] + head_g),
        (speed[0] * g[2] + speed[1] * (k[2] - push)) + (k[0] + head_k),
        speed[0] * g[3] + speed[1] * k[3] - speed[2] * push,
        energy + push,
    ]


def kernel(
    counts,
    adj_hbm, rho_hbm, vel_hbm, pre_hbm, sty_hbm, loy_hbm, chy_hbm, stx_hbm, chx_hbm, spn_hbm,
    tendency, updated,
    adj, rho, vel, pre, sty, loy, chy, stx, chx, spn,
    highs, lows, turned, other, ysend, yrecv, xsend, xrecv, twice, fy, tx, fx, tz, squares, heats,
    adj_sem, in_sem, ys_sem, yr_sem, xs_sem, xr_sem, zs_sem, zr_sem,
):
    gx, gy, gz = (lax.axis_index(n) for n in ("gx", "gy", "gz"))
    n_gx, n_gy = counts
    variables, rows_all, nz = adj.shape
    chunks = ysend.shape[1]
    rows_c = rows_all // chunks
    half = rows_c // 2
    ny = 16
    nx = rows_all // ny

    pieces = [
        pltpu.make_async_copy(
            adj_hbm.at[:, pl.ds(c * rows_c, rows_c)], adj.at[:, pl.ds(c * rows_c, rows_c)], adj_sem.at[c]
        )
        for c in range(chunks)
    ]
    loads = [
        pltpu.make_async_copy(src, dst, in_sem.at[k])
        for k, (src, dst) in enumerate(
            ((sty_hbm, sty), (stx_hbm, stx), (loy_hbm, loy), (spn_hbm, spn),
             (rho_hbm, rho), (vel_hbm, vel), (pre_hbm, pre), (chx_hbm, chx), (chy_hbm, chy))
        )
    ]
    pieces[0].start()
    loads[0].start()

    has = (gx > 0, gx < n_gx - 1, gy > 0, gy < n_gy - 1)
    edge = tuple(jnp.where(there, 0, 1) for there in has)
    to = ({"gx": gx - 1}, {"gx": gx + 1}, {"gy": gy - 1}, {"gy": gy + 1})
    partner = {"gz": 1 - gz}
    lane = lax.broadcasted_iota(jnp.int32, (rows_all, nz), 1)
    upper = lax.broadcasted_iota(jnp.int32, (8, nz), 0) < 4
    own_rest = tuple(jnp.logical_not(there) if THIN else True for there in has)
    barrier = pltpu.get_barrier_semaphore()
    for there, where in zip(has, to):

        @pl.when(there)
        def _(where=where):
            pl.semaphore_signal(barrier, inc=1, device_id=where, device_id_type=pl.DeviceIdType.MESH)

    pl.semaphore_signal(barrier, inc=1, device_id=partner, device_id_type=pl.DeviceIdType.MESH)
    for load in pieces[1:] + loads[1:]:
        load.start()
    neighbours = sum(jnp.where(there, 1, 0) for there in has) + 1

    def remote(src, dst, send, recv, where):
        return pltpu.make_async_remote_copy(
            src_ref=src, dst_ref=dst, send_sem=send, recv_sem=recv,
            device_id=where, device_id_type=pl.DeviceIdType.MESH,
        )

    def y_copy(slot, c):
        return remote(
            ysend.at[slot, c, :, pl.ds(0, SENT)], yrecv.at[1 - slot, c, :, pl.ds(0, SENT)], ys_sem.at[slot, c], yr_sem.at[1 - slot, c], to[2 + slot]
        )

    def x_copy(slot, v):
        return remote(
            xsend.at[slot, v], xrecv.at[1 - slot, v], xs_sem.at[slot, v], xr_sem.at[1 - slot, v], to[slot]
        )

    def z_copy(v):
        return remote(adj_hbm.at[v], other.at[v], zs_sem.at[v], zr_sem.at[v], partner)

    def y_part(c):
        rows = pl.ds(c * rows_c, rows_c)
        left = jnp.concatenate([sty[0, edge[2]], sty[1, edge[3]]], axis=0)
        k = sty.shape[2]
        for v in range(variables):
            high, low = split(adj[v, rows])
            highs[v, rows] = high
            lows[v, rows] = low
            right = jnp.concatenate([column(high[:half], low[:half]), column(high[half:], low[half:])], axis=1)
            full = dot(left, right)
            for slot in range(2):
                pair, rest = full[slot * k : slot * k + 8], full[slot * k + 8 : (slot + 1) * k]
                ysend[slot, c, v, :8] = pair[:, :nz]
                ysend[slot, c, v, 8:16] = pair[:, nz:]
                ysend[slot, c, v, 16:24] = jnp.where(upper | own_rest[2 + slot], rest[:, :nz], rest[:, nz:])
                ysend[slot, c, v, 24:] = rest[:, nz:]
        if c == 0:
            pl.semaphore_wait(barrier, neighbours)
        for slot in range(2):

            @pl.when(has[2 + slot])
            def _(slot=slot):
                y_copy(slot, c).start()

            @pl.when(jnp.logical_not(has[2 + slot]))
            def _(slot=slot):
                yrecv[slot, c] = ysend[slot, c]

    pieces[0].wait()
    loads[0].wait()
    y_part(0)
    for v in range(variables):
        z_copy(v).start()
    for c in range(1, chunks):
        pieces[c].wait()
    loads[1].wait()
    loads[2].wait()

    @pl.loop(0, variables)
    def _(v):
        left = jnp.concatenate([stx[0, edge[0]], stx[1, edge[1]]], axis=0)
        k = stx.shape[2]
        for q in range(ny // 4):
            halves = []
            for b in range(2):
                lines = [adj[v, pl.ds(4 * q + 2 * b + j, nx, stride=ny)] for j in range(2)]
                halves.append(jnp.concatenate(split(jnp.concatenate(lines, axis=0)), axis=0))
            lined = jnp.concatenate(halves, axis=1)
            turned[v, q] = lined
            full = dot(left, jnp.concatenate([lined, lined], axis=0))
            for b in range(2):
                lanes = slice(b * nz, (b + 1) * nz)
                xsend[0, v, 2 * q + b] = full[:k, lanes]
                xsend[1, v, 2 * q + b] = full[k : 2 * k, lanes]
        for slot in range(2):

            @pl.when(has[slot])
            def _(slot=slot):
                x_copy(slot, v).start()

            @pl.when(jnp.logical_not(has[slot]))
            def _(slot=slot):
                xrecv[slot, v] = xsend[slot, v]

    for c in range(1, chunks):
        y_part(c)

    for load in loads[3:]:
        load.wait()
    for c in range(chunks):
        rows = pl.ds(c * rows_c, rows_c)
        for v in range(variables):
            high, low = highs[v, rows], lows[v, rows]
            full = dot(
                loy[...],
                jnp.concatenate([column(high[:half], low[:half]), column(high[half:], low[half:])], axis=1),
            )
            for b in range(2):
                lanes = slice(b * nz, (b + 1) * nz)
                to_rows = pl.ds(c * rows_c + b * half, half)
                twice[v, to_rows] = full[:half, lanes]
                fy[v, to_rows] = full[half:, lanes]

    for v in range(variables):
        z_copy(v).wait_recv()

    for v in range(variables):
        theirs = other[v]
        at_low = pltpu.roll(theirs, 2 * EDGE, 1)
        at_low = at_low - at_low.astype(BF16).astype(F32)
        ends = jnp.where((lane >= EDGE) & (lane < 3 * EDGE), at_low, theirs)
        ends = jnp.where((lane >= 3 * EDGE) & (lane < 5 * EDGE), pltpu.roll(theirs, 4 * EDGE, 1), ends).astype(BF16)
        high = highs[v]
        full = dot(jnp.concatenate([high, lows[v]], axis=1), spn[0]) + dot(
            jnp.concatenate([high, ends], axis=1), spn[1]
        )
        tz[v] = full[:, :nz]
        other[v] = full[:, nz:]

    tile = 2 * ny

    @pl.loop(0, rows_all // tile)
    def _(t):
        at = pl.ds(pl.multiple_of(t * tile, tile), tile)
        speed = [vel[d, at] for d in range(3)]
        square = 0.5 * (speed[0] * speed[0] + speed[1] * speed[1] + speed[2] * speed[2])
        heat = (1.0 + 1.0 / GAMMA_LESS) * pre[at] / rho[at] + square
        squares[at] = square
        heats[at] = heat
        gained = pull([other[v, at] for v in range(5)], 2, speed, square, heat)
        for v in range(5):
            tz[v, at] += gained[v]

    def y_fix(c):
        rows = pl.ds(c * rows_c, rows_c)
        for slot in range(2):

            @pl.when(has[2 + slot])
            def _(slot=slot):
                y_copy(1 - slot, c).wait_recv()

        for v in range(variables):
            parts = ([], [])
            for slot in range(2):
                rest, last = yrecv[slot, c, v, 16:24], yrecv[slot, c, v, 24:]
                parts[0].extend([yrecv[slot, c, v, :8], jnp.where(upper | own_rest[2 + slot], rest, 0.0)])
                parts[1].extend(
                    [yrecv[slot, c, v, 8:16], jnp.where(own_rest[2 + slot], last, jnp.where(upper, 0.0, rest))]
                )
            columns = [column(*split(jnp.concatenate(part, axis=0))) for part in parts]
            full = dot(chy[edge[2], edge[3]], jnp.concatenate(columns, axis=1))
            for b in range(2):
                lanes = slice(b * nz, (b + 1) * nz)
                to_rows = pl.ds(c * rows_c + b * half, half)
                twice[v, to_rows] += full[:half, lanes]
                fy[v, to_rows] += full[half:, lanes]

    def combine(c):
        @pl.loop(0, rows_c // tile)
        def _(t):
            at = pl.ds(pl.multiple_of(c * rows_c + t * tile, tile), tile)
            first_line = c * (rows_c // ny) + t * (tile // ny)

            def natural(ref, v):
                return jnp.concatenate(
                    [ref[v, pl.ds(first_line + j, ny, stride=nx)] for j in range(tile // ny)], axis=0
                )

            speed = [vel[d, at] for d in range(3)]
            square, heat = squares[at], heats[at]
            gain = pull_two(
                [natural(fx, v) for v in range(5)], [fy[v, at] for v in range(5)], speed, square, heat
            )
            for v in range(5):
                total = (twice[v, at] + natural(tx, v)) + (tz[v, at] + gain[v])
                tendency[v, at] = 0.5 * total
                updated[v, at] = adj[v, at] + 0.25 * total

    y_fix(0)

    @pl.loop(0, variables)
    def _(v):
        for slot in range(2):

            @pl.when(has[slot])
            def _(slot=slot):
                x_copy(1 - slot, v).wait_recv()

        left = chx[edge[0], edge[1]]
        for q in range(ny // 4):
            columns = [
                column(*split(jnp.concatenate([xrecv[slot, v, 2 * q + b] for slot in range(2)], axis=0)))
                for b in range(2)
            ]
            lined = turned[v, q]
            full = dot(left, jnp.concatenate([lined, lined, jnp.concatenate(columns, axis=1)], axis=0))
            for b in range(2):
                lanes = slice(b * nz, (b + 1) * nz)
                to_rows = pl.ds((4 * q + 2 * b) * nx, 2 * nx)
                tx[v, to_rows] = full[: 2 * nx, lanes]
                fx[v, to_rows] = full[2 * nx :, lanes]

    combine(0)
    for c in range(1, chunks):
        y_fix(c)
        combine(c)

    for slot in range(2):
        for c in range(chunks):

            @pl.when(has[2 + slot])
            def _(slot=slot, c=c):
                y_copy(slot, c).wait_send()

        for v in range(variables):

            @pl.when(has[slot])
            def _(slot=slot, v=v):
                x_copy(slot, v).wait_send()

    for v in range(variables):
        z_copy(v).wait_send()


def finish(tendency, updated, tendency_hbm, updated_hbm, sem):
    writes = [
        pltpu.make_async_copy(src.at[v], dst.at[v], sem.at[k, v])
        for v in range(tendency.shape[0])
        for k, (src, dst) in enumerate(((tendency, tendency_hbm), (updated, updated_hbm)))
    ]
    for write in writes:
        write.start()
    for write in writes:
        write.wait()


def on_device(counts, adjoint, base_density, base_velocity, base_pressure):
    variables, nx, ny, nz = adjoint.shape
    chunks = 3
    rows = nx * ny
    operators = tables(nx, ny, nz)
    field = (variables, rows, nz)
    y_shape = (2, chunks, variables, 8 * RANK, nz)
    x_shape = (2, variables, ny // 2, 2 * RANK, nz)
    dma = pltpu.SemaphoreType.DMA
    hbm = pl.BlockSpec(memory_space=pl.ANY)
    whole = pltpu.VMEM(field, F32)
    whole_low = pltpu.VMEM(field, BF16)
    cells = pltpu.VMEM((rows, nz), F32)
    tendency, updated = pl.pallas_call(
        functools.partial(kernel, counts),
        out_shape=[pltpu.VMEM(field, F32)] * 2,
        in_specs=[hbm] * 10,
        out_specs=[pl.BlockSpec(memory_space=pltpu.VMEM)] * 2,
        scratch_shapes=[
            whole,
            cells,
            pltpu.VMEM((3, rows, nz), F32),
            cells,
            *[pltpu.VMEM(m.shape, BF16) for m in operators],
            whole_low,
            whole_low,
            pltpu.VMEM((variables, ny // 4, 4 * nx, 2 * nz), BF16),
            whole,
            pltpu.VMEM(y_shape, F32),
            pltpu.VMEM(y_shape, F32),
            pltpu.VMEM(x_shape, F32),
            pltpu.VMEM(x_shape, F32),
            whole,
            whole,
            whole,
            whole,
            whole,
            cells,
            cells,
            dma((chunks,)),
            dma((9,)),
            dma((2, chunks)),
            dma((2, chunks)),
            dma((2, variables)),
            dma((2, variables)),
            dma((variables,)),
            dma((variables,)),
        ],
        compiler_params=pltpu.CompilerParams(
            collective_id=0, has_side_effects=True, vmem_limit_bytes=32 << 20
        ),
        name="adjoint_step",
    )(
        *[
            pltpu.with_memory_space_constraint(jnp.asarray(x), pltpu.HBM)
            for x in (
                adjoint.reshape(field),
                base_density.reshape(rows, nz),
                base_velocity.reshape(3, rows, nz),
                base_pressure.reshape(rows, nz),
                *operators,
            )
        ]
    )
    tendency, updated = pl.pallas_call(
        finish,
        out_shape=[jax.ShapeDtypeStruct(field, F32)] * 2,
        in_specs=[pl.BlockSpec(memory_space=pltpu.VMEM)] * 2,
        out_specs=[hbm] * 2,
        scratch_shapes=[dma((2, variables))],
        compiler_params=pltpu.CompilerParams(vmem_limit_bytes=16 << 20),
        name="finish",
    )(*[pltpu.with_memory_space_constraint(x, pltpu.VMEM) for x in (tendency, updated)])
    return tendency.reshape(adjoint.shape), updated.reshape(adjoint.shape)


def solution(mesh):
    placed = (
        P(None, "gx", "gy", "gz"),
        P("gx", "gy", "gz"),
        P(None, "gx", "gy", "gz"),
        P("gx", "gy", "gz"),
    )
    return jax.shard_map(
        functools.partial(on_device, (mesh.shape["gx"], mesh.shape["gy"])),
        mesh=mesh,
        in_specs=placed,
        out_specs=(P(None, "gx", "gy", "gz"), P(None, "gx", "gy", "gz")),
        check_vma=False,
    )
```

time: 14 us -> 13.2 us (0.943)
  Pallas kernels: 13.2 us -> 12.4 us
    pallas_call x1, Pallas kernels: 12 us -> 11.1 us  [on_device(): pl.pallas_call(functools.partial(kernel, counts), out_shape=[pltpu.VMEM(f...]
where the time goes in v3:
time: 13.2 us; the launch traced here: 13.1 us
  Pallas kernels  12.4 us (94%)
  between operations  0.64 us (5%)
    pallas_call x1, Pallas kernels, on_device(): pl.pallas_call(functools.partial(kernel, counts), out_shape=[pltpu.VMEM(f...  11.1 us
    pallas_call x1, Pallas kernels, on_device(): pl.pallas_call(finish, out_shape=[jax.ShapeDtypeStruct(field, F32)] * 2,...  1.35 us

profile of v3, /device:TPU:24, one launch (start us, length us, event | category | flops | bytes accessed | tf_op | source)
XLA Modules:
  0.0 13.1 jit_solution(15438329082320480071)
XLA Ops:
  0.6 11.1 %adjoint_step.1 = (f32[5,384,128]{2,1,0:T(8,128)S(1)}, f32[5,384,128]{2,1,0:T(8,128)S(1)}) custom-call(f32[5,384,128]{2,1,0:T(8,128)} %bitcast.6, f32[384,128]{1,0:T(8,128)} %bitcast.8, f32[3,384,128]{2,1,0:T(8,128)} %bitcast.7, f32[384,128]{1,0:T(8,128)} %bitcast.9, bf16[2,2,16,256]{3,2,1,0:T(8,128)(2,1)} %constant.12.clone.sty_hbm, ...), custom_call_target="tpu_custom_call" | custom-call | tf_op jit(solution)/shard_map/adjoint_step/pallas_call | solution.py:460
  11.7 1.3 %finish.1 = (f32[5,384,128]{2,1,0:T(8,128)}, f32[5,384,128]{2,1,0:T(8,128)}) custom-call(f32[5,384,128]{2,1,0:T(8,128)S(1)} %get-tuple-element.6.tendency, f32[5,384,128]{2,1,0:T(8,128)S(1)} %get-tuple-element.7.updated), custom_call_target="tpu_custom_call" | custom-call | tf_op jit(solution)/shard_map/finish/pallas_call | solution.py:511

commit v4 on v3

--- a/solution.py
+++ b/solution.py
@@ -115,7 +115,7 @@
 @functools.lru_cache(maxsize=None)
 def tables(nx, ny, nz):
     state_y, local_y, change_y, _ = direction(ny, 4, THIN)
-    state_x, _, _, both_x = direction(nx, 2, False)
+    state_x, _, _, both_x = direction(nx, 2, THIN)
     return state_y, local_y, change_y, state_x, both_x, span_table(nz)
 
 
@@ -197,6 +197,30 @@
     lane = lax.broadcasted_iota(jnp.int32, (rows_all, nz), 1)
     upper = lax.broadcasted_iota(jnp.int32, (8, nz), 0) < 4
     own_rest = tuple(jnp.logical_not(there) if THIN else True for there in has)
+    sub = lax.broadcasted_iota(jnp.int32, (8, nz), 0)
+
+    def pack(found):
+        ahead = [pltpu.roll(f, 4, 0) if h % 2 else f for h, f in enumerate(found)]
+        pairs = [jnp.where(sub < 4, ahead[2 * p], ahead[2 * p + 1]) for p in range(4)]
+        thirds = [
+            jnp.where(
+                sub < 4,
+                jnp.where(sub < 2, ahead[g + 1], ahead[g + 3]),
+                jnp.where(sub < 6, ahead[g], ahead[g + 2]),
+            )
+            for g in (0, 4)
+        ]
+        return pairs + thirds
+
+    def unpack(slot, v, h):
+        low = 2 * ((h % 4) // 2) + 4 * (1 - h % 2)
+        mine = sub >= 4 if h % 2 else sub < 4
+        third = jnp.where((sub >= low) & (sub < low + 2), xrecv[slot, v, 4 + h // 4], 0.0)
+        got = jnp.where(mine, xrecv[slot, v, h // 2], third)
+        if h % 2:
+            got = pltpu.roll(got, 4, 0)
+        return jnp.where(own_rest[slot], xrecv[slot, v, h], got)
+
     barrier = pltpu.get_barrier_semaphore()
     for there, where in zip(has, to):
 
@@ -222,7 +246,7 @@
 
     def x_copy(slot, v):
         return remote(
-            xsend.at[slot, v], xrecv.at[1 - slot, v], xs_sem.at[slot, v], xr_sem.at[1 - slot, v], to[slot]
+            xsend.at[slot, v, pl.ds(0, 6)], xrecv.at[1 - slot, v, pl.ds(0, 6)], xs_sem.at[slot, v], xr_sem.at[1 - slot, v], to[slot]
         )
 
     def z_copy(v):
@@ -268,6 +292,7 @@
 
     @pl.loop(0, variables)
     def _(v):
+        found = ([], [])
         left = jnp.concatenate([stx[0, edge[0]], stx[1, edge[1]]], axis=0)
         k = stx.shape[2]
         for q in range(ny // 4):
@@ -279,9 +304,13 @@
             turned[v, q] = lined
             full = dot(left, jnp.concatenate([lined, lined], axis=0))
             for b in range(2):
-                lanes = slice(b * nz, (b + 1) * nz)
-                xsend[0, v, 2 * q + b] = full[:k, lanes]
-                xsend[1, v, 2 * q + b] = full[k : 2 * k, lanes]
+                for slot in range(2):
+                    found[slot].append(full[slot * k : (slot + 1) * k, b * nz : (b + 1) * nz])
+        for slot in range(2):
+            for at, packed in enumerate(pack(found[slot])):
+                xsend[slot, v, at] = jnp.where(own_rest[slot], found[slot][at], packed)
+            for at in range(6, 8):
+                xsend[slot, v, at] = found[slot][at]
         for slot in range(2):
 
             @pl.when(has[slot])
@@ -365,6 +394,33 @@
                 twice[v, to_rows] += full[:half, lanes]
                 fy[v, to_rows] += full[half:, lanes]
 
+    def take_y(c):
+        @pl.loop(0, rows_c // tile)
+        def _(t):
+            at = pl.ds(pl.multiple_of(c * rows_c + t * tile, tile), tile)
+            speed = [vel[d, at] for d in range(3)]
+            gain = pull([fy[v, at] for v in range(5)], 1, speed, squares[at], heats[at])
+            for v in range(5):
+                tz[v, at] += twice[v, at] + gain[v]
+
+    def take_x(c):
+        @pl.loop(0, rows_c // tile)
+        def _(t):
+            at = pl.ds(pl.multiple_of(c * rows_c + t * tile, tile), tile)
+            first_line = c * (rows_c // ny) + t * (tile // ny)
+
+            def natural(ref, v):
+                return jnp.concatenate(
+                    [ref[v, pl.ds(first_line + j, ny, stride=nx)] for j in range(tile // ny)], axis=0
+                )
+
+            speed = [vel[d, at] for d in range(3)]
+            gain = pull([natural(fx, v) for v in range(5)], 0, speed, squares[at], heats[at])
+            for v in range(5):
+                total = (tz[v, at] + natural(tx, v)) + gain[v]
+                tendency[v, at] = 0.5 * total
+                updated[v, at] = adj[v, at] + 0.25 * total
+
     def combine(c):
         @pl.loop(0, rows_c // tile)
         def _(t):
@@ -387,6 +443,7 @@
                 updated[v, at] = adj[v, at] + 0.25 * total
 
     y_fix(0)
+    take_y(0)
 
     @pl.loop(0, variables)
     def _(v):
@@ -399,7 +456,7 @@
         left = chx[edge[0], edge[1]]
         for q in range(ny // 4):
             columns = [
-                column(*split(jnp.concatenate([xrecv[slot, v, 2 * q + b] for slot in range(2)], axis=0)))
+                column(*split(jnp.concatenate([unpack(slot, v, 2 * q + b) for slot in range(2)], axis=0)))
                 for b in range(2)
             ]
             lined = turned[v, q]
@@ -410,7 +467,7 @@
                 tx[v, to_rows] = full[: 2 * nx, lanes]
                 fx[v, to_rows] = full[2 * nx :, lanes]
 
-    combine(0)
+    take_x(0)
     for c in range(1, chunks):
         y_fix(c)
         combine(c)

time: 13.2 us -> 13 us (0.985)
  Pallas kernels: 12.4 us -> 12.2 us
    pallas_call x1, Pallas kernels: 11.1 us -> 10.9 us  [on_device(): pl.pallas_call(functools.partial(kernel, counts), out_shape=[pltpu.VMEM(f...]
where the time goes in v4:
time: 13 us; the launch traced here: 12.9 us
  Pallas kernels  12.2 us (94%)
  between operations  0.64 us (5%)
    pallas_call x1, Pallas kernels, on_device(): pl.pallas_call(functools.partial(kernel, counts), out_shape=[pltpu.VMEM(f...  10.9 us
    pallas_call x1, Pallas kernels, on_device(): pl.pallas_call(finish, out_shape=[jax.ShapeDtypeStruct(field, F32)] * 2,...  1.35 us

profile of v4, /device:TPU:24, one launch (start us, length us, event | category | flops | bytes accessed | tf_op | source)
XLA Modules:
  0.0 12.9 jit_solution(18084553375299920242)
XLA Ops:
  0.6 10.9 %adjoint_step.1 = (f32[5,384,128]{2,1,0:T(8,128)S(1)}, f32[5,384,128]{2,1,0:T(8,128)S(1)}) custom-call(f32[5,384,128]{2,1,0:T(8,128)} %bitcast.6, f32[384,128]{1,0:T(8,128)} %bitcast.8, f32[3,384,128]{2,1,0:T(8,128)} %bitcast.7, f32[384,128]{1,0:T(8,128)} %bitcast.9, bf16[2,2,16,256]{3,2,1,0:T(8,128)(2,1)} %constant.12.clone.sty_hbm, ...), custom_call_target="tpu_custom_call" | custom-call | tf_op jit(solution)/shard_map/adjoint_step/pallas_call | solution.py:517
  11.5 1.3 %finish.1 = (f32[5,384,128]{2,1,0:T(8,128)}, f32[5,384,128]{2,1,0:T(8,128)}) custom-call(f32[5,384,128]{2,1,0:T(8,128)S(1)} %get-tuple-element.6.tendency, f32[5,384,128]{2,1,0:T(8,128)S(1)} %get-tuple-element.7.updated), custom_call_target="tpu_custom_call" | custom-call | tf_op jit(solution)/shard_map/finish/pallas_call | solution.py:568

commit v5 on v4

--- a/solution.py
+++ b/solution.py
@@ -268,8 +268,8 @@
                 ysend[slot, c, v, 8:16] = pair[:, nz:]
                 ysend[slot, c, v, 16:24] = jnp.where(upper | own_rest[2 + slot], rest[:, :nz], rest[:, nz:])
                 ysend[slot, c, v, 24:] = rest[:, nz:]
-        if c == 0:
-            pl.semaphore_wait(barrier, neighbours)
+
+    def y_send(c):
         for slot in range(2):
 
             @pl.when(has[2 + slot])
@@ -283,13 +283,17 @@
     pieces[0].wait()
     loads[0].wait()
     y_part(0)
-    for v in range(variables):
-        z_copy(v).start()
     for c in range(1, chunks):
         pieces[c].wait()
     loads[1].wait()
     loads[2].wait()
 
+    y_part(1)
+    pl.semaphore_wait(barrier, neighbours)
+    y_send(0)
+    y_send(1)
+    for v in range(variables):
+        z_copy(v).start()
     @pl.loop(0, variables)
     def _(v):
         found = ([], [])
@@ -321,8 +325,9 @@
             def _(slot=slot):
                 xrecv[slot, v] = xsend[slot, v]
 
-    for c in range(1, chunks):
+    for c in range(2, chunks):
         y_part(c)
+        y_send(c)
 
     for load in loads[3:]:
         load.wait()
@@ -442,9 +447,6 @@
                 tendency[v, at] = 0.5 * total
                 updated[v, at] = adj[v, at] + 0.25 * total
 
-    y_fix(0)
-    take_y(0)
-
     @pl.loop(0, variables)
     def _(v):
         for slot in range(2):
@@ -467,8 +469,7 @@
                 tx[v, to_rows] = full[: 2 * nx, lanes]
                 fx[v, to_rows] = full[2 * nx :, lanes]
 
-    take_x(0)
-    for c in range(1, chunks):
+    for c in range(chunks):
         y_fix(c)
         combine(c)
 
@@ -491,8 +492,7 @@
 
 def finish(tendency, updated, tendency_hbm, updated_hbm, sem):
     writes = [
-        pltpu.make_async_copy(src.at[v], dst.at[v], sem.at[k, v])
-        for v in range(tendency.shape[0])
+        pltpu.make_async_copy(src, dst, sem.at[k])
         for k, (src, dst) in enumerate(((tendency, tendency_hbm), (updated, updated_hbm)))
     ]
     for write in writes:
@@ -570,7 +570,7 @@
         out_shape=[jax.ShapeDtypeStruct(field, F32)] * 2,
         in_specs=[pl.BlockSpec(memory_space=pltpu.VMEM)] * 2,
         out_specs=[hbm] * 2,
-        scratch_shapes=[dma((2, variables))],
+        scratch_shapes=[dma((2,))],
         compiler_params=pltpu.CompilerParams(vmem_limit_bytes=16 << 20),
         name="finish",
     )(*[pltpu.with_memory_space_constraint(x, pltpu.VMEM) for x in (tendency, updated)])

time: 13 us -> 12.8 us (0.985)
  no operation moved by 1% of the time
where the time goes in v5:
time: 12.8 us; the launch traced here: 12.7 us
  Pallas kernels  12.1 us (95%)
  between operations  0.64 us (5%)
    pallas_call x1, Pallas kernels, on_device(): pl.pallas_call(functools.partial(kernel, counts), out_shape=[pltpu.VMEM(f...  10.8 us
    pallas_call x1, Pallas kernels, on_device(): pl.pallas_call(finish, out_shape=[jax.ShapeDtypeStruct(field, F32)] * 2,...  1.29 us

profile of v5, /device:TPU:24, one launch (start us, length us, event | category | flops | bytes accessed | tf_op | source)
XLA Modules:
  0.0 12.7 jit_solution(13318155804852917306)
XLA Ops:
  0.6 10.8 %adjoint_step.1 = (f32[5,384,128]{2,1,0:T(8,128)S(1)}, f32[5,384,128]{2,1,0:T(8,128)S(1)}) custom-call(f32[5,384,128]{2,1,0:T(8,128)} %bitcast.6, f32[384,128]{1,0:T(8,128)} %bitcast.8, f32[3,384,128]{2,1,0:T(8,128)} %bitcast.7, f32[384,128]{1,0:T(8,128)} %bitcast.9, bf16[2,2,16,256]{3,2,1,0:T(8,128)(2,1)} %constant.12.clone.sty_hbm, ...), custom_call_target="tpu_custom_call" | custom-call | tf_op jit(solution)/shard_map/adjoint_step/pallas_call | solution.py:517
  11.4 1.3 %finish.1 = (f32[5,384,128]{2,1,0:T(8,128)}, f32[5,384,128]{2,1,0:T(8,128)}) custom-call(f32[5,384,128]{2,1,0:T(8,128)S(1)} %get-tuple-element.6.tendency, f32[5,384,128]{2,1,0:T(8,128)S(1)} %get-tuple-element.7.updated), custom_call_target="tpu_custom_call" | custom-call | tf_op jit(solution)/shard_map/finish/pallas_call | solution.py:568

commit v6 on v5

--- a/solution.py
+++ b/solution.py
@@ -447,6 +447,8 @@
                 tendency[v, at] = 0.5 * total
                 updated[v, at] = adj[v, at] + 0.25 * total
 
+    y_fix(0)
+
     @pl.loop(0, variables)
     def _(v):
         for slot in range(2):
@@ -469,7 +471,8 @@
                 tx[v, to_rows] = full[: 2 * nx, lanes]
                 fx[v, to_rows] = full[2 * nx :, lanes]
 
-    for c in range(chunks):
+    combine(0)
+    for c in range(1, chunks):
         y_fix(c)
         combine(c)
 

time: 12.8 us -> 13.1 us (1.023)
  Pallas kernels: 12.1 us -> 12.3 us
    pallas_call x1, Pallas kernels: 10.8 us -> 11 us  [on_device(): pl.pallas_call(functools.partial(kernel, counts), out_shape=[pltpu.VMEM(f...]
where the time goes in v6:
time: 13.1 us; the launch traced here: 12.9 us
  Pallas kernels  12.3 us (94%)
  between operations  0.64 us (5%)
    pallas_call x1, Pallas kernels, on_device(): pl.pallas_call(functools.partial(kernel, counts), out_shape=[pltpu.VMEM(f...  11 us
    pallas_call x1, Pallas kernels, on_device(): pl.pallas_call(finish, out_shape=[jax.ShapeDtypeStruct(field, F32)] * 2,...  1.29 us

profile of v6, /device:TPU:24, one launch (start us, length us, event | category | flops | bytes accessed | tf_op | source)
XLA Modules:
  0.0 12.9 jit_solution(14734989577489303971)
XLA Ops:
  0.6 11.0 %adjoint_step.1 = (f32[5,384,128]{2,1,0:T(8,128)S(1)}, f32[5,384,128]{2,1,0:T(8,128)S(1)}) custom-call(f32[5,384,128]{2,1,0:T(8,128)} %bitcast.6, f32[384,128]{1,0:T(8,128)} %bitcast.8, f32[3,384,128]{2,1,0:T(8,128)} %bitcast.7, f32[384,128]{1,0:T(8,128)} %bitcast.9, bf16[2,2,16,256]{3,2,1,0:T(8,128)(2,1)} %constant.12.clone.sty_hbm, ...), custom_call_target="tpu_custom_call" | custom-call | tf_op jit(solution)/shard_map/adjoint_step/pallas_call | solution.py:520
  11.6 1.3 %finish.1 = (f32[5,384,128]{2,1,0:T(8,128)}, f32[5,384,128]{2,1,0:T(8,128)}) custom-call(f32[5,384,128]{2,1,0:T(8,128)S(1)} %get-tuple-element.6.tendency, f32[5,384,128]{2,1,0:T(8,128)S(1)} %get-tuple-element.7.updated), custom_call_target="tpu_custom_call" | custom-call | tf_op jit(solution)/shard_map/finish/pallas_call | solution.py:571
